TPU v7x, 32 devices: a whole 2x2x4 slice. The times are simulated.
32 devices in a mesh: fsdp: 8 (over z, y), tp: 4 (over x, core).
Axes of the slice: x: 2, y: 2, z: 4, core: 2. Of those that a mesh axis runs over, the one named last changes fastest.
Arguments:
- states: bfloat16 [8, 8, 32, 4096], P('fsdp', None, None, 'tp'), may hold values from -40 to 40
- dest: int32 [8, 8], P('fsdp'), may hold values from 0 to 7, each once within a row
- lengths: int32 [8, 8], P('fsdp'), may hold values from 1 to 32, 160 in all within a row
- strata: int32 [8, 8, 1], P('fsdp'), may hold values from 0 to 7
- ffn_gain: float32 [4096], replicated, may hold values from 0.1 to 1.9
- gate_weight: bfloat16 [4096, 7168], P('fsdp', 'tp'), may hold values from -0.0703125 to 0.0703125
- up_weight: bfloat16 [4096, 7168], P('fsdp', 'tp'), may hold values from -0.1 to 0.1
- down_weight: bfloat16 [7168, 4096], P('tp', 'fsdp'), may hold values from -0.058238643 to 0.058238643
- final_gain: float32 [4096], replicated, may hold values from 0.1 to 1.9
- value_weight: float32 [4096], replicated, may hold values from -0.09375 to 0.09375
Outputs:
- rewards: float32 [8, 8], P('fsdp')
- stratum_means: float32 [8], replicated
Inputs may be any that keep to these rules, and one draw needn't show every extreme that they name: Each row of dest is a permutation: every source group sends exactly one response to every scoring group. Each source group's lengths sum to 160. `strata`: every stratum holds at least one response.
All inputs are finite; a program needn't handle non-finite values.
Results may differ from a plain program's by a relative error of at most 0.004.
Values may be sent and summed in bfloat16 or wider, within the bound.
A program may use at most 128 MiB of HBM per device.

v0:
```python
import jax
import jax.numpy as jnp
from jax import lax
from jax.sharding import PartitionSpec as P

S = 8
epsilon = 1e-05


def body(
    states,
    dest,
    lengths,
    strata,
    ffn_gain,
    gate_weight,
    up_weight,
    down_weight,
    final_gain,
    value_weight,
):
    groups = dest.shape[1]
    length = states.shape[2]
    slots = jnp.arange(groups, dtype=jnp.int32)
    picker = (dest[0][None, :] == slots[:, None]).astype(jnp.int32)
    source_slot = jnp.sum(picker * slots[None, :], axis=1)
    outgoing = jnp.take(states[0], source_slot, axis=0)
    out_len = jnp.take(lengths[0], source_slot, axis=0)
    out_str = jnp.take(strata[0, :, 0], source_slot, axis=0)
    received, recv_len, recv_str = (
        lax.all_to_all(outgoing, "fsdp", split_axis=0, concat_axis=0, tiled=True),
        lax.all_to_all(out_len, "fsdp", split_axis=0, concat_axis=0, tiled=True),
        lax.all_to_all(out_str, "fsdp", split_axis=0, concat_axis=0, tiled=True),
    )
    gathered = lax.all_gather(received, "tp", axis=2, tiled=True)
    feature_width = gathered.shape[2]
    token_count = groups * length
    widened = gathered.reshape(token_count, feature_width).astype(jnp.float32)
    normed = (
        widened
        * lax.rsqrt(jnp.mean(widened * widened, axis=1, keepdims=True) + epsilon)
        * ffn_gain[None, :]
    ).astype(jnp.bfloat16)
    gate_full, up_full, down_full = (
        lax.all_gather(gate_weight, "fsdp", axis=0, tiled=True),
        lax.all_gather(up_weight, "fsdp", axis=0, tiled=True),
        lax.all_gather(down_weight, "fsdp", axis=1, tiled=True),
    )
    gate = jnp.dot(normed, gate_full, preferred_element_type=jnp.float32)
    up_part = jnp.dot(normed, up_full, preferred_element_type=jnp.float32)
    hidden = (jax.nn.silu(gate) * up_part).astype(jnp.bfloat16)
    partial_value = jnp.dot(hidden, down_full, preferred_element_type=jnp.float32)
    head_scale = final_gain * value_weight
    total = lax.psum(partial_value.astype(jnp.bfloat16), "tp").astype(jnp.float32)
    mixed = widened + total
    product = jnp.sum(mixed * head_scale[None, :], axis=1)
    value = product * lax.rsqrt(jnp.mean(mixed * mixed, axis=1) + epsilon)
    value = value.reshape(groups, length)
    positions = jnp.arange(length, dtype=jnp.int32)
    live_mask = (positions[None, :] < recv_len[:, None]).astype(jnp.float32)
    reward = jnp.sum(value * live_mask, axis=1) / recv_len.astype(jnp.float32)
    strata_ids = jnp.arange(S, dtype=jnp.int32)
    onehot = (recv_str[:, None] == strata_ids[None, :]).astype(jnp.float32)
    sums = jnp.sum(reward[:, None] * onehot, axis=0)
    counts = jnp.sum(onehot, axis=0)
    sums, counts = lax.psum((sums, counts), "fsdp")
    return (reward.reshape(1, groups), sums / counts)


def solution(mesh):
    return jax.shard_map(
        body,
        mesh=mesh,
        in_specs=(
            P("fsdp", None, None, "tp"),
            P("fsdp", None),
            P("fsdp", None),
            P("fsdp", None, None),
            P(),
            P("fsdp", "tp"),
            P("fsdp", "tp"),
            P("tp", "fsdp"),
            P(),
            P(),
        ),
        out_specs=(P("fsdp", None), P()),
        check_vma=False,
    )
```

profile of v0, /device:TPU:0, one launch (start us, length us, event | category | flops | bytes accessed | tf_op | source)
XLA Modules:
  0.0 764.5 jit_solution(11980279169275734645)
XLA Ops:
  7.2 0.8 select_reduce_fusion.2
  8.1 1.3 gather_fusion.2
  10.1 21.7 %all_to_all.23 = bf16[8,32,1024]{2,1,0:T(8,128)(2,1)} all-to-all(bf16[8,32,1024]{2,1,0:T(8,128)(2,1)S(1)} %broadcast_select_fusion), channel_id=1, replica_groups=mesh['fsdp'=8,'tp'=4] {'fsdp'}, dimensions={0} | all-to-all | bytes 1048576 | tf_op jit(solution)/shard_map/all_to_all | solution.py:31
  31.9 0.7 all-gather.7.cloned.1.call-update
  32.7 0.7 all-gather.11.cloned.1.call-update
  34.0 19.6 %all-gather.5.cloned.1.call-done = bf16[8,32,4096]{2,1,0:T(8,128)(2,1)} async-done(((bf16[8,32,1024]{2,1,0:T(8,128)(2,1)}), bf16[8,32,4096]{2,1,0:T(8,128)(2,1)}) %all-gather.5.cloned.1.call-update) | async-done | bytes 2097168 | tf_op jit(solution)/shard_map/all_gather | solution.py:35
  53.6 2.2 fusion
  55.9 1.9 fusion.2
  57.9 200.0 %all-gather.7.cloned.1.call-done = bf16[4096,1792]{1,0:T(8,128)(2,1)} async-done(((bf16[512,1792]{1,0:T(8,128)(2,1)}), bf16[4096,1792]{1,0:T(8,128)(2,1)}) %all-gather.7.cloned.1.call-update) | async-done | bytes 14680080 | tf_op jit(solution)/shard_map/all_gather | solution.py:45
  257.8 11.0 %fusion.6 = f32[256,1792]{1,0:T(8,128)} fusion(bf16[256,4096]{1,0:T(8,128)(2,1)} %fusion.2, bf16[4096,1792]{1,0:T(8,128)(2,1)} %all-gather.7.cloned.1.call-done), kind=kOutput, calls=%fused_computation.36 | convolution fusion | flops 3758096384 | bytes 18612224 | tf_op jit(solution)/shard_map/dot_general | solution.py:49
  268.9 191.5 %all-gather.11.cloned.1.call-done = bf16[1792,4096]{1,0:T(8,128)(2,1)} async-done(((bf16[1792,512]{1,0:T(8,128)(2,1)}), bf16[1792,4096]{1,0:T(8,128)(2,1)}) %all-gather.11.cloned.1.call-update) | async-done | bytes 14680080 | tf_op jit(solution)/shard_map/all_gather | solution.py:47
  460.4 202.3 %all-gather.9.cloned.1.call-done = bf16[4096,1792]{1,0:T(8,128)(2,1)} async-done(((bf16[512,1792]{1,0:T(8,128)(2,1)}), bf16[4096,1792]{1,0:T(8,128)(2,1)}) %all-gather.9.cloned.1.call-update) | async-done | bytes 14680080 | tf_op jit(solution)/shard_map/all_gather | solution.py:46
  662.6 20.2 %convolution_convert_fusion = bf16[256,4096]{1,0:T(8,128)(2,1)} fusion(bf16[1792,4096]{1,0:T(8,128)(2,1)} %all-gather.11.cloned.1.call-done, bf16[256,4096]{1,0:T(8,128)(2,1)} %fusion.2, bf16[4096,1792]{1,0:T(8,128)(2,1)} %all-gather.9.cloned.1.call-done, f32[256,1792]{1,0:T(8,128)} %fusion.6), kind=kOutput, calls=%fused_computation.3 | convolution fusion | flops 7519993856 | bytes 35389440 | tf_op jit(solution)/shard_map/dot_general | solution.py:52
  682.8 0.6 copy-done.1
  683.4 0.6 gather_fusion.1
  684.1 0.7 copy.16
  684.8 3.3 all-to-all-start
  688.0 0.7 copy.17
  688.7 5.7 all-to-all-done
  694.4 3.3 all-to-all-start.2
  698.0 6.2 all-to-all-done.2
  704.5 28.0 %all-reduce.3.cloned.1.call-done = bf16[256,4096]{1,0:T(8,128)(2,1)} async-done(((bf16[256,4096]{1,0:T(8,128)(2,1)}), bf16[256,4096]{1,0:T(8,128)(2,1)}) %all-reduce.3.cloned.1.call-update) | async-done | bytes 2097168 | tf_op jit(solution)/shard_map/psum | solution.py:54
  732.5 2.7 multiply_reduce_fusion
  736.1 21.4 %all-reduce = (f32[8]{0:T(128)S(1)}, f32[8]{0:T(128)S(1)}) all-reduce(f32[8]{0:T(128)S(1)} %get-tuple-element.6, f32[8]{0:T(128)S(1)} %get-tuple-element.5), channel_id=1, replica_groups=mesh['fsdp'=8,'tp'=4] {'fsdp'}, use_global_device_ids=true, to_apply=%region_7.9 | all-reduce | flops 16 | bytes 128 | tf_op jit(solution)/shard_map/psum | solution.py:66
  (40 shorter events, 3.6 us)
Async XLA Ops:
  7.2 2.2 copy-start
  7.2 46.4 %all-gather.5.cloned.1.call-start = ((), (), s32[]{:S(2)}) async-start(), calls=%async_computation.3 | async-start | bytes 2621440 | tf_op jit(solution)/shard_map/all_gather | solution.py:35
  31.9 226.0 %all-gather.7.cloned.1.call-start = ((), (), s32[]{:S(2)}) async-start(), calls=%async_computation.4 | async-start | bytes 16515072 | tf_op jit(solution)/shard_map/all_gather | solution.py:45
  32.6 427.7 %all-gather.11.cloned.1.call-start = ((), (), s32[]{:S(2)}) async-start(), calls=%async_computation.6 | async-start | bytes 16515072 | tf_op jit(solution)/shard_map/all_gather | solution.py:47
  33.3 22.6 %copy-start.3 = (f32[4096]{0:T(1024)S(1)}, f32[4096]{0:T(1024)}, u32[]{:S(2)}) copy-start(f32[4096]{0:T(1024)} %param.16) | copy-start | bytes 49156
  33.4 629.3 %all-gather.9.cloned.1.call-start = ((), (), s32[]{:S(2)}) async-start(), calls=%async_computation.5 | async-start | bytes 16515072 | tf_op jit(solution)/shard_map/all_gather | solution.py:46
  33.9 698.6 %all-reduce.3.cloned.1.call-start = ((), (), s32[]{:S(2)}) async-start(), calls=%async_computation.7 | async-start | bytes 4194304 | tf_op jit(solution)/shard_map/psum | solution.py:54
  53.6 2.3 copy-start.2
  682.8 0.7 copy-start.1
  682.8 5.9 copy-start.4
  682.8 5.9 copy-start.5
  684.8 9.7 %all-to-all-start = ((s32[8,1,1]{2,1,0:T(1,128)}), s32[8,1,1]{2,1,0:T(1,128)S(1)}, u32[]{:S(2)}, u32[]{:S(2)}) async-start(s32[8,1,1]{2,1,0:T(1,128)} %copy.16), calls=%async_computation | async-start | bytes 8192 | tf_op jit(solution)/shard_map/all_to_all | solution.py:32
  694.4 9.7 %all-to-all-start.2 = ((s32[8,1,1]{2,1,0:T(1,128)}), s32[8,1,1]{2,1,0:T(1,128)S(1)}, u32[]{:S(2)}, u32[]{:S(2)}) async-start(s32[8,1,1]{2,1,0:T(1,128)} %copy.17), calls=%async_computation.2 | async-start | bytes 8192 | tf_op jit(solution)/shard_map/all_to_all | solution.py:33
Sparse Core Ops, SparseCore 0:
  32.0 21.5 all-gather.4
  55.8 202.0 all-gather.6
  259.9 200.4 all-gather.10
  462.4 200.1 all-gather.8
  682.9 49.5 all-reduce.2
where the time goes:
time: 765 us
  waiting for transfers between devices  655 us (86%)
  blocking collectives  43.1 us (6%)
  matrix products  31.2 us (4%)
  between operations  13.9 us (2%)
  other arithmetic  9.75 us (1%)
    all_gather x1, waiting for transfers between devices, body(): lax.all_gather(up_weight, 'fsdp', axis=0, tiled=True)  202 us
    all_gather x1, waiting for transfers between devices, body(): lax.all_gather(gate_weight, 'fsdp', axis=0, tiled=True)  200 us
    all_gather x1, waiting for transfers between devices, body(): lax.all_gather(down_weight, 'fsdp', axis=1, tiled=True)  192 us
    psum x1, waiting for transfers between devices, body(): lax.psum(partial_value.astype(jnp.bfloat16), 'tp').astype(jnp.float32)  28 us
    all_to_all x1, blocking collectives, body(): lax.all_to_all(outgoing, 'fsdp', split_axis=0, concat_axis=0, tiled=True)  21.7 us
    psum x1, blocking collectives, body(): sums, counts = lax.psum((sums, counts), 'fsdp')  21.4 us
    dot_general x1, matrix products, body(): jnp.dot(hidden, down_full, preferred_element_type=jnp.float32)  20.2 us
    all_gather x1, waiting for transfers between devices, body(): gathered = lax.all_gather(received, 'tp', axis=2, tiled=True)  19.6 us
  transfers between devices with their start and end apart: 7, of which 7 were waited for; matrix products, arithmetic and copies ran while one was open for 2% of the time, Pallas kernels for 0%

commit v1 on v0

--- a/solution.py
+++ b/solution.py
@@ -32,7 +32,12 @@
         lax.all_to_all(out_len, "fsdp", split_axis=0, concat_axis=0, tiled=True),
         lax.all_to_all(out_str, "fsdp", split_axis=0, concat_axis=0, tiled=True),
     )
-    gathered = lax.all_gather(received, "tp", axis=2, tiled=True)
+    ring = [received]
+    for hop in range(3):
+        ring.append(lax.ppermute(ring[-1], "tp", [(dev, (dev + 1) % 4) for dev in range(4)]))
+    gathered = jnp.roll(
+        jnp.concatenate(ring[::-1], axis=2), (lax.axis_index("tp") + 1) * ring[0].shape[2], axis=2
+    )
     feature_width = gathered.shape[2]
     token_count = groups * length
     widened = gathered.reshape(token_count, feature_width).astype(jnp.float32)

time: 765 us -> 728 us (0.952)
  waiting for transfers between devices: 655 us -> 610 us
  blocking collectives: 43.1 us -> 54.5 us
    all_gather x1, waiting for transfers between devices: 200 us -> 146 us  [body(): lax.all_gather(gate_weight, 'fsdp', axis=0, tiled=True)]
    ppermute x0 -> x3, waiting for transfers between devices: none -> 25.8 us  [body(): lax.ppermute(ring[-1], 'tp', [(dev, (dev + 1) % 4) for dev in range(4)])]
    all_gather x1 -> x0, waiting for transfers between devices: 19.6 us -> none  [body(): gathered = lax.all_gather(received, 'tp', axis=2, tiled=True)]
    all_to_all x1, blocking collectives: 21.7 us -> 33.1 us  [body(): lax.all_to_all(outgoing, 'fsdp', split_axis=0, concat_axis=0, tiled=True)]
    all_gather x1, waiting for transfers between devices: 192 us -> 202 us  [body(): lax.all_gather(down_weight, 'fsdp', axis=1, tiled=True)]
    all_gather x1, waiting for transfers between devices: 202 us -> 194 us  [body(): lax.all_gather(up_weight, 'fsdp', axis=0, tiled=True)]
  transfers between devices with their start and end apart: 7 -> 9, of which waited for: 7 -> 9; matrix products, arithmetic and copies ran while one was open for 2% -> 2% of each run, Pallas kernels for 0% -> 0%
where the time goes in v1:
time: 728 us
  waiting for transfers between devices  610 us (84%)
  blocking collectives  54.5 us (7%)
  matrix products  28.1 us (4%)
  between operations  14 us (2%)
  other arithmetic  8.21 us (1%)
    all_gather x1, waiting for transfers between devices, body(): lax.all_gather(down_weight, 'fsdp', axis=1, tiled=True)  202 us
    all_gather x1, waiting for transfers between devices, body(): lax.all_gather(up_weight, 'fsdp', axis=0, tiled=True)  194 us
    all_gather x1, waiting for transfers between devices, body(): lax.all_gather(gate_weight, 'fsdp', axis=0, tiled=True)  146 us
    all_to_all x1, blocking collectives, body(): lax.all_to_all(outgoing, 'fsdp', split_axis=0, concat_axis=0, tiled=True)  33.1 us
    psum x1, waiting for transfers between devices, body(): lax.psum(partial_value.astype(jnp.bfloat16), 'tp').astype(jnp.float32)  28.6 us
    ppermute x3, waiting for transfers between devices, body(): lax.ppermute(ring[-1], 'tp', [(dev, (dev + 1) % 4) for dev in range(4)])  25.8 us
    psum x1, blocking collectives, body(): sums, counts = lax.psum((sums, counts), 'fsdp')  21.4 us
    dot_general x1, matrix products, body(): jnp.dot(hidden, down_full, preferred_element_type=jnp.float32)  19.6 us
  transfers between devices with their start and end apart: 9, of which 9 were waited for; matrix products, arithmetic and copies ran while one was open for 2% of the time, Pallas kernels for 0%

profile of v1, /device:TPU:0, one launch (start us, length us, event | category | flops | bytes accessed | tf_op | source)
XLA Modules:
  0.0 727.7 jit_solution(10326600088449746105)
XLA Ops:
  7.2 0.7 all-gather.4.cloned.1.call-update
  8.0 0.7 all-gather.6.cloned.1.call-update
  8.7 0.7 all-gather.8.cloned.1.call-update
  9.6 0.6 gather_fusion.2
  11.0 33.1 %all_to_all.23 = bf16[8,32,1024]{2,1,0:T(8,128)(2,1)S(1)} all-to-all(bf16[8,32,1024]{2,1,0:T(8,128)(2,1)S(1)} %broadcast_select_fusion), channel_id=1, replica_groups=mesh['fsdp'=8,'tp'=4] {'fsdp'}, dimensions={0} | all-to-all | bytes 1048576 | tf_op jit(solution)/shard_map/all_to_all | solution.py:31
  44.1 8.6 %collective-permute-done = bf16[8,32,1024]{2,1,0:T(8,128)(2,1)S(1)} collective-permute-done((bf16[8,32,1024]{2,1,0:T(8,128)(2,1)S(1)}, bf16[8,32,1024]{2,1,0:T(8,128)(2,1)S(1)}, u32[]{:S(2)}, u32[]{:S(2)}) %collective-permute-start) | collective-permute-done | bytes 524320 | tf_op jit(solution)/shard_map/ppermute | solution.py:37
  52.7 8.6 %collective-permute-done.1 = bf16[8,32,1024]{2,1,0:T(8,128)(2,1)S(1)} collective-permute-done((bf16[8,32,1024]{2,1,0:T(8,128)(2,1)S(1)}, bf16[8,32,1024]{2,1,0:T(8,128)(2,1)S(1)}, u32[]{:S(2)}, u32[]{:S(2)}) %collective-permute-start.1) | collective-permute-done | bytes 524320 | tf_op jit(solution)/shard_map/ppermute | solution.py:37
  61.3 8.6 %collective-permute-done.2 = bf16[8,32,1024]{2,1,0:T(8,128)(2,1)S(1)} collective-permute-done((bf16[8,32,1024]{2,1,0:T(8,128)(2,1)S(1)}, bf16[8,32,1024]{2,1,0:T(8,128)(2,1)S(1)}, u32[]{:S(2)}, u32[]{:S(2)}) %collective-permute-start.2) | collective-permute-done | bytes 524320 | tf_op jit(solution)/shard_map/ppermute | solution.py:37
  70.3 2.1 copy-done.3
  73.0 2.2 fusion.2
  75.2 145.7 %all-gather.4.cloned.1.call-done = bf16[4096,1792]{1,0:T(8,128)(2,1)} async-done(((bf16[512,1792]{1,0:T(8,128)(2,1)}), bf16[4096,1792]{1,0:T(8,128)(2,1)}) %all-gather.4.cloned.1.call-update) | async-done | bytes 14680080 | tf_op jit(solution)/shard_map/all_gather | solution.py:50
  220.9 8.5 %fusion.6 = f32[256,1792]{1,0:T(8,128)} fusion(bf16[256,4096]{1,0:T(8,128)(2,1)S(1)} %fusion.2, bf16[4096,1792]{1,0:T(8,128)(2,1)} %all-gather.4.cloned.1.call-done), kind=kOutput, calls=%fused_computation.44 | convolution fusion | flops 3758096384 | bytes 18612224 | tf_op jit(solution)/shard_map/dot_general | solution.py:54
  229.4 193.9 %all-gather.6.cloned.1.call-done = bf16[4096,1792]{1,0:T(8,128)(2,1)} async-done(((bf16[512,1792]{1,0:T(8,128)(2,1)}), bf16[4096,1792]{1,0:T(8,128)(2,1)}) %all-gather.6.cloned.1.call-update) | async-done | bytes 14680080 | tf_op jit(solution)/shard_map/all_gather | solution.py:51
  423.3 202.4 %all-gather.8.cloned.1.call-done = bf16[1792,4096]{1,0:T(8,128)(2,1)} async-done(((bf16[1792,512]{1,0:T(8,128)(2,1)}), bf16[1792,4096]{1,0:T(8,128)(2,1)}) %all-gather.8.cloned.1.call-update) | async-done | bytes 14680080 | tf_op jit(solution)/shard_map/all_gather | solution.py:52
  625.8 19.6 %convolution_convert_fusion = bf16[256,4096]{1,0:T(8,128)(2,1)} fusion(bf16[1792,4096]{1,0:T(8,128)(2,1)} %all-gather.8.cloned.1.call-done, bf16[256,4096]{1,0:T(8,128)(2,1)S(1)} %fusion.2, bf16[4096,1792]{1,0:T(8,128)(2,1)} %all-gather.6.cloned.1.call-done, f32[256,1792]{1,0:T(8,128)} %fusion.6), kind=kOutput, calls=%fused_computation.3 | convolution fusion | flops 7519993856 | bytes 35389440 | tf_op jit(solution)/shard_map/dot_general | solution.py:57
  646.1 0.7 copy.16
  646.8 3.3 all-to-all-start
  650.1 0.7 copy.17
  650.8 5.7 all-to-all-done
  656.5 3.3 all-to-all-start.2
  660.0 6.2 all-to-all-done.2
  666.6 28.6 %all-reduce.3.cloned.1.call-done = bf16[256,4096]{1,0:T(8,128)(2,1)} async-done(((bf16[256,4096]{1,0:T(8,128)(2,1)}), bf16[256,4096]{1,0:T(8,128)(2,1)}) %all-reduce.3.cloned.1.call-update) | async-done | bytes 2097168 | tf_op jit(solution)/shard_map/psum | solution.py:59
  695.1 3.3 multiply_reduce_fusion
  699.3 21.4 %all-reduce = (f32[8]{0:T(128)S(1)}, f32[8]{0:T(128)S(1)}) all-reduce(f32[8]{0:T(128)S(1)} %get-tuple-element.6, f32[8]{0:T(128)S(1)} %get-tuple-element.5), channel_id=1, replica_groups=mesh['fsdp'=8,'tp'=4] {'fsdp'}, use_global_device_ids=true, to_apply=%region_7.9 | all-reduce | flops 16 | bytes 128 | tf_op jit(solution)/shard_map/psum | solution.py:71
  (55 shorter events, 4.6 us)
Async XLA Ops:
  7.2 3.1 copy-start
  7.2 2.3 copy-start.7
  7.2 2.4 copy-start.1
  7.2 213.7 %all-gather.4.cloned.1.call-start = ((), (), s32[]{:S(2)}) async-start(), calls=%async_computation.3 | async-start | bytes 16515072 | tf_op jit(solution)/shard_map/all_gather | solution.py:50
  7.9 415.4 %all-gather.6.cloned.1.call-start = ((), (), s32[]{:S(2)}) async-start(), calls=%async_computation.4 | async-start | bytes 16515072 | tf_op jit(solution)/shard_map/all_gather | solution.py:51
  8.7 617.1 %all-gather.8.cloned.1.call-start = ((), (), s32[]{:S(2)}) async-start(), calls=%async_computation.5 | async-start | bytes 16515072 | tf_op jit(solution)/shard_map/all_gather | solution.py:52
  9.4 685.7 %all-reduce.3.cloned.1.call-start = ((), (), s32[]{:S(2)}) async-start(), calls=%async_computation.6 | async-start | bytes 4194304 | tf_op jit(solution)/shard_map/psum | solution.py:59
  44.1 8.6 %collective-permute-start = (bf16[8,32,1024]{2,1,0:T(8,128)(2,1)S(1)}, bf16[8,32,1024]{2,1,0:T(8,128)(2,1)S(1)}, u32[]{:S(2)}, u32[]{:S(2)}) collective-permute-start(bf16[8,32,1024]{2,1,0:T(8,128)(2,1)S(1)} %all_to_all.23), channel_id=1, source_target_pairs={{0,1},{1,2},{2,3},{3,0},{4,5},{5,6},{6,7},{7,4},{8,9},{9,10},{10,1... | collective-permute-start | bytes 1572872 | tf_op jit(solution)/shard_map/ppermute | solution.py:37
  52.7 8.6 %collective-permute-start.1 = (bf16[8,32,1024]{2,1,0:T(8,128)(2,1)S(1)}, bf16[8,32,1024]{2,1,0:T(8,128)(2,1)S(1)}, u32[]{:S(2)}, u32[]{:S(2)}) collective-permute-start(bf16[8,32,1024]{2,1,0:T(8,128)(2,1)S(1)} %collective-permute-done), channel_id=1, source_target_pairs={{0,1},{1,2},{2,3},{3,0},{4,5},{5,6},{6,7},{7,4},{8,9},{9,10},{10,1... | collective-permute-start | bytes 1572872 | tf_op jit(solution)/shard_map/ppermute | solution.py:37
  61.3 8.6 %collective-permute-start.2 = (bf16[8,32,1024]{2,1,0:T(8,128)(2,1)S(1)}, bf16[8,32,1024]{2,1,0:T(8,128)(2,1)S(1)}, u32[]{:S(2)}, u32[]{:S(2)}) collective-permute-start(bf16[8,32,1024]{2,1,0:T(8,128)(2,1)S(1)} %collective-permute-done.1), channel_id=1, source_target_pairs={{0,1},{1,2},{2,3},{3,0},{4,5},{5,6},{6,7},{7,4},{8,9},{9,10},{10,1... | collective-permute-start | bytes 1572872 | tf_op jit(solution)/shard_map/ppermute | solution.py:37
  70.0 3.0 copy-start.4
  70.3 2.1 copy-start.3
  229.4 416.0 %copy-start.2 = (s32[1,8]{1,0:T(1,128)S(1)}, s32[1,8]{1,0:T(1,128)}, u32[]{:S(2)}) copy-start(s32[1,8]{1,0:T(1,128)} %param.14) | copy-start | bytes 100
  229.4 421.4 %copy-start.5 = (f32[4096]{0:T(1024)S(1)}, f32[4096]{0:T(1024)}, u32[]{:S(2)}) copy-start(f32[4096]{0:T(1024)} %param.20) | copy-start | bytes 49156
  229.4 421.4 %copy-start.6 = (f32[4096]{0:T(1024)S(1)}, f32[4096]{0:T(1024)}, u32[]{:S(2)}) copy-start(f32[4096]{0:T(1024)} %param.21) | copy-start | bytes 49156
  646.8 9.7 %all-to-all-start = ((s32[8,1,1]{2,1,0:T(1,128)}), s32[8,1,1]{2,1,0:T(1,128)S(1)}, u32[]{:S(2)}, u32[]{:S(2)}) async-start(s32[8,1,1]{2,1,0:T(1,128)} %copy.16), calls=%async_computation | async-start | bytes 8192 | tf_op jit(solution)/shard_map/all_to_all | solution.py:32
  656.5 9.7 %all-to-all-start.2 = ((s32[8,1,1]{2,1,0:T(1,128)}), s32[8,1,1]{2,1,0:T(1,128)S(1)}, u32[]{:S(2)}, u32[]{:S(2)}) async-start(s32[8,1,1]{2,1,0:T(1,128)} %copy.17), calls=%async_computation.2 | async-start | bytes 8192 | tf_op jit(solution)/shard_map/all_to_all | solution.py:33
Sparse Core Ops, SparseCore 0:
  10.2 210.6 all-gather.3
  223.1 200.1 all-gather.5
  425.4 200.3 all-gather.7
  645.6 49.5 all-reduce.2
